TPU v7x, 256 devices: a whole 4x4x8 slice. The times are simulated.
256 devices in a mesh: row: 8 (over z_lo, y), col: 32 (over x, z_hi, core).
Axes of the slice: x: 4, y: 4, z: 8 (z_hi: 4, z_lo: 2; z = z_hi * 2 + z_lo), core: 2. Of those that a mesh axis runs over, the one named last changes fastest.
Arguments:
- object_field: float32 [2, 2, 3072, 12288], P(None, None, 'row', 'col'), may hold values from -5 to 5
- offsets: int32 [32, 32, 2], P('row', 'col'), may hold values from 0 to 256
- amplitudes: float32 [32, 32, 256, 256], P('row', 'col'), may hold values from 0.3 to 3
- probe: float32 [2, 256, 256], replicated, may hold values from -5 to 5
- phase: float32 [256, 256], replicated, may hold values from -3.140625 to 3.140625
Outputs:
- object_grad: float32 [2, 2, 3072, 12288], P(None, None, 'row', 'col')
- probe_grad: float32 [2, 256, 256], replicated
All inputs are finite; a program needn't handle non-finite values.
Results may differ from a plain program's by a relative error of at most 0.0003.
Values sent between devices are 32-bit elements; how exact they have to be, the bound alone decides.
A program may use at most 64 MiB of HBM per device.

v0:
```python
import math

import jax
import jax.numpy as jnp
from jax import lax
from jax.sharding import PartitionSpec as P

HALO = 64


HIGH = lax.Precision.HIGHEST


def padded(block, sides, width):
    for axis, dim in sides:
        count = lax.axis_size(axis)
        forward = [(i, i + 1) for i in range(count - 1)]
        forward.append((count - 1, 0))
        backward = [(target, source) for source, target in forward]
        low = lax.ppermute(
            lax.slice_in_dim(block, block.shape[dim] - width, None, axis=dim), axis, forward
        )
        high = lax.ppermute(lax.slice_in_dim(block, 0, width, axis=dim), axis, backward)
        block = jnp.concatenate([low, block, high], axis=dim)
    return block


def in_one(arrays, axis):
    line, at, finished = (jnp.concatenate([a.reshape(-1) for a in arrays]), 0, [])
    subtotal = lax.psum(line, axis)
    for a in arrays:
        finished.append(subtotal[at : at + a.size].reshape(a.shape))
        at += a.size
    return tuple(finished)


def mixing(count, sign):
    index = jnp.arange(count, dtype=jnp.int32)
    product = index[:, None] * index[None, :] % count
    angle = product.astype(jnp.float32) * (2.0 * math.pi / count)
    factor = 1.0 / math.sqrt(count)
    cosine = jnp.cos(angle) * factor
    sine = jnp.sin(angle) * factor * sign
    real_row = jnp.stack([cosine, -sine])
    imag_row = jnp.stack([sine, cosine])
    return jnp.stack([real_row, imag_row])


def transform(table, field):
    first = jnp.einsum("dckn,pcnm->pdkm", table, field, precision=HIGH)
    return jnp.einsum("pcnm,dckm->pdnk", first, table, precision=HIGH)


def local(object_field, offsets, amplitudes, probe, phase):
    slices = object_field.shape[0]
    size = probe.shape[1]
    count = offsets.shape[0]
    widened = padded(object_field, (("row", 2), ("col", 3)), HALO)
    extended = [widened[s] for s in range(slices)]
    row_off = offsets[:, 0, 0]
    col_off = offsets[:, 0, 1]
    forward_table = mixing(size, -1.0)
    inverse_table = mixing(size, 1.0)
    prop_re = jnp.cos(phase)
    prop_im = jnp.sin(phase)
    psi = jnp.broadcast_to(probe[None], (count, 2, size, size))
    wins = []
    psis = []
    exit_wave = psi
    for s in range(slices):
        field = extended[s]

        def cut(start_r, start_c):
            return lax.dynamic_slice(field, (0, start_r, start_c), (2, size, size))

        window = jax.vmap(cut)(row_off, col_off)
        wins.append(window)
        psis.append(psi)
        exit_wave = jnp.stack(
            [
                psi[:, 0] * window[:, 0] - psi[:, 1] * window[:, 1],
                psi[:, 0] * window[:, 1] + psi[:, 1] * window[:, 0],
            ],
            axis=1,
        )
        if s < slices - 1:
            freq = transform(forward_table, exit_wave)
            moved = jnp.stack(
                [
                    freq[:, 0] * prop_re - freq[:, 1] * prop_im,
                    freq[:, 0] * prop_im + freq[:, 1] * prop_re,
                ],
                axis=1,
            )
            psi = transform(inverse_table, moved)
    far = transform(forward_table, exit_wave)
    magnitude = jnp.sqrt(far[:, 0] * far[:, 0] + far[:, 1] * far[:, 1])
    keep = 1.0 - amplitudes[:, 0] / jnp.maximum(magnitude, 0.5)
    back = transform(inverse_table, far * keep[:, None])
    grads = [None] * slices
    probe_re = None
    probe_im = None
    for s in range(slices - 1, -1, -1):
        wave = psis[s]
        grads[s] = jnp.stack(
            [
                wave[:, 0] * back[:, 0] + wave[:, 1] * back[:, 1],
                wave[:, 0] * back[:, 1] - wave[:, 1] * back[:, 0],
            ],
            axis=1,
        )
        window = wins[s]
        conj_re = window[:, 0] * back[:, 0] + window[:, 1] * back[:, 1]
        conj_im = window[:, 0] * back[:, 1] - window[:, 1] * back[:, 0]
        if s > 0:
            freq = transform(forward_table, jnp.stack([conj_re, conj_im], axis=1))
            moved = jnp.stack(
                [
                    freq[:, 0] * prop_re + freq[:, 1] * prop_im,
                    freq[:, 1] * prop_re - freq[:, 0] * prop_im,
                ],
                axis=1,
            )
            back = transform(inverse_table, moved)
        else:
            probe_re = jnp.sum(conj_re, axis=0)
            probe_im = jnp.sum(conj_im, axis=0)
    stacked = jnp.stack(grads, axis=1)
    span = extended[0].shape[1]
    tile = span - 2 * HALO

    def add_window(index, gathered):
        start_r = row_off[index]
        start_c = col_off[index]
        current = lax.dynamic_slice(gathered, (0, 0, start_r, start_c), (slices, 2, size, size))
        return lax.dynamic_update_slice(
            gathered, current + stacked[index], (0, 0, start_r, start_c)
        )

    gathered = lax.fori_loop(0, count, add_window, jnp.zeros((slices, 2, span, span), jnp.float32))
    row_rims = jnp.concatenate(
        [gathered[:, :, 0:HALO, :], gathered[:, :, span - HALO : span, :]], axis=2
    )
    row_back = padded(row_rims, (("row", 2),), HALO)
    inner = gathered[:, :, HALO : HALO + tile, :]
    inner = inner.at[:, :, 0:HALO, :].add(row_back[:, :, 0:HALO, :])
    inner = inner.at[:, :, tile - HALO : tile, :].add(row_back[:, :, 3 * HALO : 4 * HALO, :])
    col_rims = jnp.concatenate([inner[:, :, :, 0:HALO], inner[:, :, :, span - HALO : span]], axis=3)
    col_back = padded(col_rims, (("col", 3),), HALO)
    result = inner[:, :, :, HALO : HALO + tile]
    result = result.at[:, :, :, 0:HALO].add(col_back[:, :, :, 0:HALO])
    result = result.at[:, :, :, tile - HALO : tile].add(col_back[:, :, :, 3 * HALO : 4 * HALO])
    total_re, total_im = in_one((probe_re, probe_im), ("row", "col"))
    everyone = count * lax.axis_size("row") * lax.axis_size("col")
    factor = 1.0 / math.sqrt(everyone)
    probe_grad = jnp.stack([total_re, total_im]) * factor
    return (result, probe_grad)


def solution(mesh):
    in_specs = (
        P(None, None, "row", "col"),
        P("row", "col", None),
        P("row", "col", None, None),
        P(),
        P(),
    )
    out_specs = (P(None, None, "row", "col"), P())
    return jax.shard_map(local, mesh=mesh, in_specs=in_specs, out_specs=out_specs, check_vma=False)
```

profile of v0, /device:TPU:1, one launch (start us, length us, event | category | flops | bytes accessed | tf_op | source)
XLA Modules:
  0.0 545.5 jit_solution(14628427916170283784)
XLA Ops:
  29.1 3.8 collective-permute-start.2
  43.3 5.2 collective-permute-done.3
  54.8 18.4 %while.21 = (s32[]{:T(128)}, f32[2,512,512]{1,2,0:T(8,128)}, s32[4,3]{1,0:T(4,128)S(1)}, f32[4,2,256,256]{2,3,1,0:T(8,128)}, s32[]{:T(128)}) while((s32[]{:T(128)}, f32[2,512,512]{1,2,0:T(8,128)}, s32[4,3]{1,0:T(4,128)S(1)}, f32[4,2,256,256]{2,3,1,0:T(8,128)}, s32[]{:T(128)}) %tuple.115), condition=%wide.while_cond.5, body=%wide.while_body.5.sunk | while | flops 2 | bytes 4194929 | solution.py:74
  75.0 3.5 fusion
  78.5 3.6 fusion.27
  82.4 3.5 fusion.25
  85.9 15.3 %fusion.36 = f32[4,2,256,256]{2,3,1,0:T(8,128)} fusion(f32[4,256,2,256,1]{3,1,4,2,0:T(8,128)S(1)} %fusion.25, f32[1,2,256,256]{3,2,1,0:T(8,128)S(1)} %get-tuple-element.282, f32[1,2,256,256]{3,2,1,0:T(8,128)S(1)} %get-tuple-element.279), kind=kOutput, calls=%fused_computation.50 | convolution fusion | flops 3221487616 | bytes 5242880 | tf_op jit(solution)/shard_map/pcnm,dckm->pdnk/dot_general | solution.py:51
  102.7 18.1 %while.20 = (s32[]{:T(128)}, f32[2,512,512]{1,2,0:T(8,128)}, s32[4,3]{1,0:T(4,128)S(1)}, f32[4,2,256,256]{2,3,1,0:T(8,128)}, s32[]{:T(128)}) while((s32[]{:T(128)}, f32[2,512,512]{1,2,0:T(8,128)}, s32[4,3]{1,0:T(4,128)S(1)}, f32[4,2,256,256]{2,3,1,0:T(8,128)}, s32[]{:T(128)}) %tuple.126), condition=%wide.while_cond.4, body=%wide.while_body.4.sunk | while | flops 2 | bytes 4194929 | solution.py:74
  126.9 3.6 fusion.30
  131.0 3.5 fusion.23
  134.5 4.0 fusion.39
  143.5 3.6 fusion.33
  147.3 3.7 fusion.21
  151.0 3.6 fusion.42
  166.3 81.9 %while.19 = (s32[]{:T(128)}, f32[2,2,512,512]{3,2,1,0:T(8,128)}, s32[4]{0:T(128)S(1)}, s32[4]{0:T(128)S(1)}, f32[4,2,2,256,256]{3,4,2,0,1:T(8,128)}, /*index=5*/s32[]{:T(128)}, s32[]{:T(128)}, s32[]{:T(128)}) while((s32[]{:T(128)}, f32[2,2,512,512]{3,2,1,0:T(8,128)}, s32[4]{0:T(128)S(1)}, s32[4]{0:T(128)S(1)}, ...), condition=%wide.region_1.2_spmd, body=%wide.region_0.1_spmd.sunk | while | flops 262152 | bytes 9437377 | solution.py:140
  174.8 12.3 %dynamic_update_slice.8 = f32[2,2,512,512]{3,2,1,0:T(8,128)} dynamic-update-slice(f32[2,2,512,512]{3,2,1,0:T(8,128)} %get-tuple-element.421, f32[2,2,256,256]{3,2,1,0:T(8,128)S(1)} %bitcast_add_fusion.2, s32[]{:T(128)} %constant.160.clone.1..sunk, s32[]{:T(128)} %constant.160.clone.1..sunk, s32[]{:T(128)S(6)} %select_n.115, s32[]{:T(128)S(6)} %select_n.116) | dynamic-update-slice | bytes 2097156 | tf_op jit(solution)/shard_map/while/body/eval_jaxpr/dynamic_update_slice | solution.py:136
  195.6 12.1 %dynamic_update_slice.8 = f32[2,2,512,512]{3,2,1,0:T(8,128)} dynamic-update-slice(f32[2,2,512,512]{3,2,1,0:T(8,128)} %get-tuple-element.421, f32[2,2,256,256]{3,2,1,0:T(8,128)S(1)} %bitcast_add_fusion.2, s32[]{:T(128)} %constant.160.clone.1..sunk, s32[]{:T(128)} %constant.160.clone.1..sunk, s32[]{:T(128)S(6)} %select_n.115, s32[]{:T(128)S(6)} %select_n.116) | dynamic-update-slice | bytes 2097156 | tf_op jit(solution)/shard_map/while/body/eval_jaxpr/dynamic_update_slice | solution.py:136
  216.2 11.4 %dynamic_update_slice.8 = f32[2,2,512,512]{3,2,1,0:T(8,128)} dynamic-update-slice(f32[2,2,512,512]{3,2,1,0:T(8,128)} %get-tuple-element.421, f32[2,2,256,256]{3,2,1,0:T(8,128)S(1)} %bitcast_add_fusion.2, s32[]{:T(128)} %constant.160.clone.1..sunk, s32[]{:T(128)} %constant.160.clone.1..sunk, s32[]{:T(128)S(6)} %select_n.115, s32[]{:T(128)S(6)} %select_n.116) | dynamic-update-slice | bytes 2097156 | tf_op jit(solution)/shard_map/while/body/eval_jaxpr/dynamic_update_slice | solution.py:136
  236.1 12.0 %dynamic_update_slice.8 = f32[2,2,512,512]{3,2,1,0:T(8,128)} dynamic-update-slice(f32[2,2,512,512]{3,2,1,0:T(8,128)} %get-tuple-element.421, f32[2,2,256,256]{3,2,1,0:T(8,128)S(1)} %bitcast_add_fusion.2, s32[]{:T(128)} %constant.160.clone.1..sunk, s32[]{:T(128)} %constant.160.clone.1..sunk, s32[]{:T(128)S(6)} %select_n.115, s32[]{:T(128)S(6)} %select_n.116) | dynamic-update-slice | bytes 2097156 | tf_op jit(solution)/shard_map/while/body/eval_jaxpr/dynamic_update_slice | solution.py:136
  250.4 3.6 collective-permute-start.5
  257.1 8.6 %collective-permute-done.4 = f32[2,2,64,512]{3,2,1,0:T(8,128)} collective-permute-done((f32[2,2,64,512]{3,2,1,0:T(8,128)}, f32[2,2,64,512]{3,2,1,0:T(8,128)}, u32[]{:S(2)}, u32[]{:S(2)}) %collective-permute-start.4) | collective-permute-done | bytes 524320 | tf_op jit(solution)/shard_map/ppermute | solution.py:20
  271.8 239.2 %all-reduce.2.cloned.1.call-done = f32[131072]{0:T(1024)} async-done(((f32[131072]{0:T(1024)}), f32[131072]{0:T(1024)}) %all-reduce.2.cloned.1.call-update) | async-done | bytes 524304 | tf_op jit(solution)/shard_map/psum | solution.py:30
  528.1 3.9 scatter-add.16
  534.7 3.7 scatter-add.19
  (180 shorter events, 151.2 us)
Async XLA Ops:
  7.2 503.8 %all-reduce.2.cloned.1.call-start = ((), (), s32[]{:S(2)}) async-start(), calls=%async_computation | async-start | bytes 1048576 | tf_op jit(solution)/shard_map/psum | solution.py:30
  8.4 15.0 %collective-permute-start = (f32[2,2,64,384]{3,2,1,0:T(8,128)S(1)}, f32[2,2,64,384]{3,2,1,0:T(8,128)}, u32[]{:S(2)}, u32[]{:S(2)}) collective-permute-start(f32[2,2,64,384]{3,2,1,0:T(8,128)S(1)} %get-tuple-element.271), channel_id=1, source_target_pairs={{0,32},{32,64},{64,96},{96,128},{128,160},{160,192},{192,224},{224... | collective-permute-start | bytes 1179656 | tf_op jit(solution)/shard_map/ppermute | solution.py:20
  10.6 14.0 %collective-permute-start.1 = (f32[2,2,64,384]{3,2,1,0:T(8,128)S(1)}, f32[2,2,64,384]{3,2,1,0:T(8,128)}, u32[]{:S(2)}, u32[]{:S(2)}) collective-permute-start(f32[2,2,64,384]{3,2,1,0:T(8,128)S(1)} %get-tuple-element.272), channel_id=1, source_target_pairs={{32,0},{64,32},{96,64},{128,96},{160,128},{192,160},{224,192},{0,2... | collective-permute-start | bytes 1179656 | tf_op jit(solution)/shard_map/ppermute | solution.py:23
  17.8 3.9 copy-start.17
  19.9 9.3 %copy-start = (f32[2,2,384,384]{2,3,1,0:T(8,128)}, f32[2,2,384,384]{2,3,1,0:T(8,128)S(1)}, u32[]{:S(2)}) copy-start(f32[2,2,384,384]{2,3,1,0:T(8,128)S(1)} %copy.81) | copy-start | bytes 7077892
  29.1 10.5 %copy-start.13 = (f32[4,1,256,256]{3,2,1,0:T(8,128)S(1)}, f32[4,1,256,256]{3,2,1,0:T(8,128)}, u32[]{:S(2)}) copy-start(f32[4,1,256,256]{3,2,1,0:T(8,128)} %param.17) | copy-start | bytes 3145732
  29.1 14.1 %collective-permute-start.2 = (f32[2,2,512,64]{2,3,1,0:T(8,128)}, f32[2,2,512,64]{2,3,1,0:T(8,128)}, u32[]{:S(2)}, u32[]{:S(2)}) collective-permute-start(f32[2,2,512,64]{2,3,1,0:T(8,128)} %get-tuple-element.259), channel_id=1, source_target_pairs={{0,1},{1,2},{2,3},{3,4},{4,5},{5,6},{6,7},{7,8},{8,9},{9,10},{10,1... | collective-permute-start | bytes 1572872 | tf_op jit(solution)/shard_map/ppermute | solution.py:20
  33.0 15.5 %collective-permute-start.3 = (f32[2,2,512,64]{2,3,1,0:T(8,128)}, f32[2,2,512,64]{2,3,1,0:T(8,128)}, u32[]{:S(2)}, u32[]{:S(2)}) collective-permute-start(f32[2,2,512,64]{2,3,1,0:T(8,128)} %get-tuple-element.260), channel_id=1, source_target_pairs={{1,0},{2,1},{3,2},{4,3},{5,4},{6,5},{7,6},{8,7},{9,8},{10,9},{11,1... | collective-permute-start | bytes 1572872 | tf_op jit(solution)/shard_map/ppermute | solution.py:23
  34.2 7.8 %copy-start.16 = (f32[1,256,256]{2,1,0:T(8,128)S(1)}, f32[1,256,256]{2,1,0:T(8,128)}, u32[]{:S(2)}) copy-start(f32[1,256,256]{2,1,0:T(8,128)} %fusion.70) | copy-start | bytes 786436
  41.0 7.5 %copy-start.1 = (f32[2,2,384,384]{2,3,1,0:T(8,128)S(1)}, f32[2,2,384,384]{2,3,1,0:T(8,128)}, u32[]{:S(2)}) copy-start(f32[2,2,384,384]{2,3,1,0:T(8,128)} %copy-done) | copy-start | bytes 7077892
  41.0 7.5 %copy-start.5 = (f32[2,2,64,384]{2,3,1,0:T(8,128)S(1)}, f32[2,2,64,384]{2,3,1,0:T(8,128)}, u32[]{:S(2)}) copy-start(f32[2,2,64,384]{2,3,1,0:T(8,128)} %copy.82) | copy-start | bytes 1179652
  78.5 3.6 copy-start.9
  78.5 3.6 copy-start.11
  134.5 4.1 copy-start.2
  134.5 4.1 copy-start.3
  143.5 3.6 copy-start.10
  143.5 3.6 copy-start.12
  151.0 3.6 copy-start.4
  248.1 5.9 %copy-start.14 = (f32[32,2,8,128]{3,1,2,0:T(2,128)S(1)}, f32[32,2,8,128]{3,1,2,0:T(2,128)}, u32[]{:S(2)}) copy-start(f32[32,2,8,128]{3,1,2,0:T(2,128)} %copy.168) | copy-start | bytes 786436
  248.1 5.9 %copy-start.15 = (f32[32,2,8,128]{3,1,2,0:T(2,128)S(1)}, f32[32,2,8,128]{3,1,2,0:T(2,128)}, u32[]{:S(2)}) copy-start(f32[32,2,8,128]{3,1,2,0:T(2,128)} %copy.169) | copy-start | bytes 786436
  250.4 15.3 %collective-permute-start.4 = (f32[2,2,64,512]{3,2,1,0:T(8,128)}, f32[2,2,64,512]{3,2,1,0:T(8,128)}, u32[]{:S(2)}, u32[]{:S(2)}) collective-permute-start(f32[2,2,64,512]{3,2,1,0:T(8,128)} %get-tuple-element.250), channel_id=1, source_target_pairs={{0,32},{32,64},{64,96},{96,128},{128,160},{160,192},{192,224},{224... | collective-permute-start | bytes 1572872 | tf_op jit(solution)/shard_map/ppermute | solution.py:20
  250.4 16.6 %collective-permute-start.5 = (f32[2,2,64,512]{3,2,1,0:T(8,128)}, f32[2,2,64,512]{3,2,1,0:T(8,128)}, u32[]{:S(2)}, u32[]{:S(2)}) collective-permute-start(f32[2,2,64,512]{3,2,1,0:T(8,128)} %get-tuple-element.249), channel_id=1, source_target_pairs={{32,0},{64,32},{96,64},{128,96},{160,128},{192,160},{224,192},{0,2... | collective-permute-start | bytes 1572872 | tf_op jit(solution)/shard_map/ppermute | solution.py:23
  271.8 251.9 %collective-permute-start.6 = (f32[2,2,384,64]{2,3,1,0:T(8,128)}, f32[2,2,384,64]{2,3,1,0:T(8,128)}, u32[]{:S(2)}, u32[]{:S(2)}) collective-permute-start(f32[2,2,384,64]{2,3,1,0:T(8,128)} %copy.108), channel_id=1, source_target_pairs={{0,1},{1,2},{2,3},{3,4},{4,5},{5,6},{6,7},{7,8},{8,9},{9,10},{10,1... | collective-permute-start | bytes 1179656 | tf_op jit(solution)/shard_map/ppermute | solution.py:20
  517.7 14.4 %collective-permute-start.7 = (f32[2,2,384,64]{2,3,1,0:T(8,128)}, f32[2,2,384,64]{2,3,1,0:T(8,128)}, u32[]{:S(2)}, u32[]{:S(2)}) collective-permute-start(f32[2,2,384,64]{2,3,1,0:T(8,128)} %copy.110), channel_id=1, source_target_pairs={{1,0},{2,1},{3,2},{4,3},{5,4},{6,5},{7,6},{8,7},{9,8},{10,9},{11,1... | collective-permute-start | bytes 1179656 | tf_op jit(solution)/shard_map/ppermute | solution.py:23
  (4 other events, 8.3 us)
Sparse Core Ops, SparseCore 0:
  257.2 253.6 all-reduce.1
where the time goes:
time: 554 us; the launch traced here: 545 us
  waiting for transfers between devices  253 us (46%)
  local copies, waits for them, and re-layouts  154 us (28%)
  matrix products  54.7 us (10%)
  other arithmetic  38.1 us (7%)
  loops' own time  16 us (3%)
  starting transfers between devices  14.7 us (3%)
  between operations  14.7 us (3%)
    psum x1, waiting for transfers between devices, in_one(): subtotal = lax.psum(line, axis)  239 us
    dynamic_update_slice x4, local copies, waits for them, and re-layouts, add_window(): lax.dynamic_update_slice(gathered, current + stacked[index], (0, 0, start...  47.8 us
    gather x48, local copies, waits for them, and re-layouts  36.1 us
    dot_general x6, matrix products, transform(): return jnp.einsum('pcnm,dckm->pdnk', first, table, precision=HIGH)  33.6 us
    dot_general x6, matrix products, transform(): first = jnp.einsum('dckn,pcnm->pdkm', table, field, precision=HIGH)  21.1 us
    another operation x1, loops' own time, local(): lax.fori_loop(0, count, add_window, jnp.zeros((slices, 2, span, span), jn...  15.6 us
  transfers between devices with their start and end apart: 9, of which 3 were waited for; matrix products, arithmetic and copies ran while one was open for 9% of the time, Pallas kernels for 0%

commit v1 on v0

v1 whole, which is shorter than its diff:
```python
import math, functools
import numpy as np
import jax, jax.numpy as jnp
from jax import lax
from jax.experimental import pallas as pl
from jax.experimental.pallas import tpu as pltpu
import ml_dtypes
from jax.sharding import PartitionSpec as P

TILE=384; HALO=64; N=256; H=128; POS=4
F32=jnp.float32; BF=jnp.bfloat16

def tables():
    k=np.arange(H)[:,None].astype(np.int64); n=np.arange(H)[None,:].astype(np.int64)
    out=[]
    for odd in (0,1):
        ang=-2*np.pi*(((2*k+odd)*n)%N)/N
        c=np.cos(ang)/16; s=np.sin(ang)/16
        out.append(np.block([[c,-s],[s,c]]))
    fe,fo=out
    t=np.stack([fe,fo,fe.T,fo.T]).astype(np.float32)
    hi=t.astype(ml_dtypes.bfloat16)
    lo=(t-hi.astype(np.float32)).astype(ml_dtypes.bfloat16)
    perm=np.zeros((N,N),np.float32)
    idx=np.concatenate([np.arange(0,N,2),np.arange(1,N,2)])
    perm[np.arange(N),idx]=1
    pm=np.stack([perm,perm.T]).astype(ml_dtypes.bfloat16)
    return hi,lo,pm

def split(x):
    hi=x.astype(BF); lo=(x-hi.astype(F32)).astype(BF)
    return hi,lo

def mm(a,b):
    return jnp.dot(a,b,preferred_element_type=F32)

def left(th,tl,x):
    xh,xl=split(x)
    return mm(jnp.concatenate([th,th,tl],1), jnp.concatenate([xh,xl,xh],0))
def right(x,th,tl):
    xh,xl=split(x)
    return mm(jnp.concatenate([xh,xl,xh],1), jnp.concatenate([th,th,tl],0))

def fwd(t,re,im):
    hi,lo=t
    a=jnp.concatenate([re[:H]+re[H:],im[:H]+im[H:]],0)
    b=jnp.concatenate([re[:H]-re[H:],im[:H]-im[H:]],0)
    ye=left(hi[0],lo[0],a); yo=left(hi[1],lo[1],b)
    re=jnp.concatenate([ye[:H],yo[:H]],0); im=jnp.concatenate([ye[H:],yo[H:]],0)
    a=jnp.concatenate([re[:,:H]+re[:,H:],im[:,:H]+im[:,H:]],1)
    b=jnp.concatenate([re[:,:H]-re[:,H:],im[:,:H]-im[:,H:]],1)
    ye=right(a,hi[2],lo[2]); yo=right(b,hi[3],lo[3])
    return jnp.concatenate([ye[:,:H],yo[:,:H]],1), jnp.concatenate([ye[:,H:],yo[:,H:]],1)

def inv(t,re,im):
    hi,lo=t
    u=right(jnp.concatenate([re[:,:H],im[:,:H]],1),hi[0],lo[0])
    v=right(jnp.concatenate([re[:,H:],im[:,H:]],1),hi[1],lo[1])
    s=u+v; d=u-v
    re=jnp.concatenate([s[:,:H],d[:,:H]],1); im=jnp.concatenate([s[:,H:],d[:,H:]],1)
    u=left(hi[2],lo[2],jnp.concatenate([re[:H],im[:H]],0))
    v=left(hi[3],lo[3],jnp.concatenate([re[H:],im[H:]],0))
    s=u+v; d=u-v
    return jnp.concatenate([s[:H],d[:H]],0), jnp.concatenate([s[H:],d[H:]],0)

def split3(x):
    h=x.astype(BF); r=x-h.astype(F32); m=r.astype(BF); l=(r-m.astype(F32)).astype(BF)
    return h,m,l
def permute(pm,x):
    h,m,l=split3(x)
    y=mm(pm[0],h)+mm(pm[0],m)+mm(pm[0],l)
    h,m,l=split3(y)
    return mm(h,pm[1])+mm(m,pm[1])+mm(l,pm[1])

def compute_kernel(off_ref, obj_ref, ns_ref, ew_ref, co_ref, amp_ref, probe_ref, phase_ref, hi_ref, lo_ref, pm_ref,
                   gt_ref, gns_ref, gew_ref, gco_ref, pg_ref,
                   ext, gext, hc, hs):
    lane64=lax.broadcasted_iota(jnp.int32,(1,128),1)<64
    for s in range(2):
        for c in range(2):
            ext[s,c,0:TILE,0:TILE]=obj_ref[s,c]
            ext[s,c,TILE:512,0:TILE]=ns_ref[s,c]
            p0=ew_ref[s,0,c]; p1=ew_ref[s,1,c]
            ext[s,c,0:192,TILE:512]=jnp.where(lane64,p0,pltpu.roll(p1,64,1))
            ext[s,c,192:384,TILE:512]=jnp.where(lane64,pltpu.roll(p0,64,1),p1)
            for h in range(2):
                cr=co_ref[s,2*h]; cl=co_ref[s,2*h+1]
                if c==0: blk=jnp.where(lane64,cr,pltpu.roll(cl,64,1))
                else: blk=jnp.where(lane64,pltpu.roll(cr,64,1),cl)
                ext[s,c,TILE+64*h:TILE+64*h+64,TILE:512]=blk
    gext[...]=jnp.zeros_like(gext)
    pg_ref[...]=jnp.zeros_like(pg_ref)
    pm=(pm_ref[0],pm_ref[1])
    ph=permute(pm,phase_ref[...])
    hc[...]=jnp.cos(ph); hs[...]=jnp.sin(ph)
    t=([hi_ref[i] for i in range(4)],[lo_ref[i] for i in range(4)])
    rows=lax.broadcasted_iota(jnp.int32,(N,1),0); cols=lax.broadcasted_iota(jnp.int32,(1,N),1)

    def one(p):
        r=off_ref[p,0]; c=off_ref[p,1]
        ra=(rows>=r-64)&(rows<r+192); ca=(cols>=c-64)&(cols<c+192)
        rm=jnp.broadcast_to(ra,(N,N)); cm=jnp.broadcast_to(ca,(N,N))
        def window(s,k):
            e=ext.at[s,k]
            return jnp.where(rm,jnp.where(cm,e[0:N,0:N],e[0:N,N:512]),jnp.where(cm,e[N:512,0:N],e[N:512,N:512]))
        sr=lax.rem(r+192,N); sc=lax.rem(c+192,N)
        br=lax.rem(N-sr,N); bc=lax.rem(N-sc,N)
        def roll(x,a,b):
            return pltpu.roll(pltpu.roll(x,a,0),b,1)
        def scatter(s,k,g):
            e=gext.at[s,k]
            z=jnp.zeros_like(g)
            gr=jnp.where(rm,g,z); gb=jnp.where(rm,z,g)
            e[0:N,0:N]+=jnp.where(cm,gr,z); e[0:N,N:512]+=jnp.where(cm,z,gr)
            e[N:512,0:N]+=jnp.where(cm,gb,z); e[N:512,N:512]+=jnp.where(cm,z,gb)
        pr=roll(probe_ref[0],sr,sc); pi=roll(probe_ref[1],sr,sc)
        wr=window(0,0); wi=window(0,1)
        fr,fi=fwd(t,pr*wr-pi*wi,pr*wi+pi*wr)
        cc=hc[...]; ss=hs[...]
        qr,qi=inv(t,fr*cc-fi*ss,fr*ss+fi*cc)
        wr=window(1,0); wi=window(1,1)
        fr,fi=fwd(t,qr*wr-qi*wi,qr*wi+qi*wr)
        keep=1.0-permute(pm,amp_ref[p])*lax.rsqrt(jnp.maximum(fr*fr+fi*fi,0.25))
        br_,bi_=inv(t,fr*keep,fi*keep)
        scatter(1,0,qr*br_+qi*bi_); scatter(1,1,qr*bi_-qi*br_)
        fr,fi=fwd(t,wr*br_+wi*bi_,wr*bi_-wi*br_)
        cc=hc[...]; ss=hs[...]
        br_,bi_=inv(t,fr*cc+fi*ss,fi*cc-fr*ss)
        scatter(0,0,pr*br_+pi*bi_); scatter(0,1,pr*bi_-pi*br_)
        wr=window(0,0); wi=window(0,1)
        pg_ref[0]+=roll(wr*br_+wi*bi_,br,bc)
        pg_ref[1]+=roll(wr*bi_-wi*br_,br,bc)

    def pair(i,_):
        one(2*i); one(2*i+1)
        return 0
    lax.fori_loop(0,POS//2,pair,0)
    for s in range(2):
        for c in range(2):
            gt_ref[s,c]=gext[s,c,0:TILE,0:TILE]
            gns_ref[s,c]=gext[s,c,TILE:512,0:TILE]
            gew_ref[s,c]=gext[s,c,0:TILE,TILE:512]
            gco_ref[s,c]=gext[s,c,TILE:512,TILE:512]

def compute(off,obj,ns,ew,co,amp,probe,phase,interpret=False):
    hi,lo,pm=tables()
    V=pl.BlockSpec(memory_space=pltpu.VMEM)
    return pl.pallas_call(compute_kernel,
        out_shape=[jax.ShapeDtypeStruct(s,F32) for s in [(2,2,TILE,TILE),(2,2,128,TILE),(2,2,TILE,128),(2,2,128,128),(2,N,N)]],
        in_specs=[pl.BlockSpec(memory_space=pltpu.SMEM)]+[V]*10, out_specs=[V]*5,
        scratch_shapes=[pltpu.VMEM((2,2,512,512),F32)]*2+[pltpu.VMEM((N,N),F32)]*2,
        compiler_params=pltpu.CompilerParams(vmem_limit_bytes=60<<20),
        interpret=interpret,
    )(off,obj,ns,ew,co,amp,probe,phase,jnp.asarray(hi),jnp.asarray(lo),jnp.asarray(pm))


MESH=pl.DeviceIdType.MESH


def place():
    a=lax.axis_index("row"); b=lax.axis_index("col")
    nr=lax.axis_size("row"); nc=lax.axis_size("col")
    return a,b,nr,nc


def greet(partners):
    bar=pltpu.get_barrier_semaphore()
    for d in partners:
        pl.semaphore_signal(bar,inc=1,device_id=d,device_id_type=MESH)
    pl.semaphore_wait(bar,len(partners))


def around(a,b,nr,nc):
    up=lax.rem(a+nr-1,nr); dn=lax.rem(a+1,nr); lf=lax.rem(b+nc-1,nc); rt=lax.rem(b+1,nc)
    return up,dn,lf,rt


def halo_kernel(obj_ref, ns_ref, ew_ref, co_ref, pe, pc, ssem, rsem):
    a,b,nr,nc=place()
    up,dn,lf,rt=around(a,b,nr,nc)
    low=lax.broadcasted_iota(jnp.int32,(1,128),1)<64
    greet([(up,b),(dn,b),(a,lf),(a,rt),(up,lf),(up,rt),(dn,lf),(dn,rt)])
    copies=[]
    def send(src,dst,dev):
        i=len(copies)
        c=pltpu.make_async_remote_copy(src,dst,ssem.at[i],rsem.at[i],device_id=dev,device_id_type=MESH)
        c.start(); copies.append(c)
    for s in range(2):
        send(obj_ref.at[s,:,0:64,:],ns_ref.at[s,:,0:64,:],(up,b))
        send(obj_ref.at[s,:,TILE-64:TILE,:],ns_ref.at[s,:,64:128,:],(dn,b))
        for c in range(2):
            x=obj_ref[s,c,:,0:128]; y=obj_ref[s,c,:,256:384]
            pe[s,0,c]=jnp.where(low,x[0:192],pltpu.roll(x[192:384],64,1))
            pe[s,1,c]=jnp.where(low,pltpu.roll(y[0:192],64,1),y[192:384])
        for h in range(2):
            r0=(TILE-64)*h
            pc[s,2*h]=jnp.where(low,obj_ref[s,0,r0:r0+64,0:128],pltpu.roll(obj_ref[s,1,r0:r0+64,0:128],64,1))
            pc[s,2*h+1]=jnp.where(low,pltpu.roll(obj_ref[s,0,r0:r0+64,256:384],64,1),obj_ref[s,1,r0:r0+64,256:384])
        send(pe.at[s,0],ew_ref.at[s,0],(a,lf))
        send(pe.at[s,1],ew_ref.at[s,1],(a,rt))
        for h,rr in ((0,up),(1,dn)):
            for l,cc in ((0,lf),(1,rt)):
                send(pc.at[s,2*h+l],co_ref.at[s,2*h+l],(rr,cc))
    for c in copies: c.wait()


def halos(obj):
    V=pl.BlockSpec(memory_space=pltpu.VMEM)
    return pl.pallas_call(halo_kernel,
        out_shape=[jax.ShapeDtypeStruct(s,F32) for s in [(2,2,128,TILE),(2,2,2,192,128),(2,4,64,128)]],
        in_specs=[V],out_specs=[V]*3,
        scratch_shapes=[pltpu.VMEM((2,2,2,192,128),F32),pltpu.VMEM((2,4,64,128),F32),
                        pltpu.SemaphoreType.DMA((16,)),pltpu.SemaphoreType.DMA((16,))],
        compiler_params=pltpu.CompilerParams(collective_id=0,has_side_effects=True,vmem_limit_bytes=30<<20),
    )(obj)


def return_kernel(scale, gt_ref, gns_ref, gew_ref, gco_ref, pg_ref, out_ref, pout_ref,
                  pe, pc, rns, rew, rco, half, w1, q1, w2, q2, w3, q3, ag2, ssem, rsem):
    a,b,nr,nc=place()
    up,dn,lf,rt=around(a,b,nr,nc)
    core=lax.rem(b,2); zh=lax.rem(b//2,4); x=b//8
    mate=b+1-2*core
    rows=[lax.rem(a+k,nr) for k in range(1,8)]
    xs=[lax.rem(x+k,4) for k in range(1,4)]
    zs=[lax.rem(zh+k,4) for k in range(1,4)]
    low=lax.broadcasted_iota(jnp.int32,(1,128),1)<64
    greet([(r,b) for r in rows]+[(a,lf),(a,rt),(up,lf),(up,rt),(dn,lf),(dn,rt)]
          +[(a,xx*8+lax.rem(b,8)) for xx in xs]+[(a,x*8+zz*2+core) for zz in zs])
    count=[0]; pend=[]
    def send(src,dst,dev):
        i=count[0]; count[0]+=1
        c=pltpu.make_async_remote_copy(src,dst,ssem.at[i],rsem.at[i],device_id=dev,device_id_type=MESH)
        c.start(); pend.append(c)
        return c
    s1=send(pg_ref.at[1-core],half,(a,mate))
    ret=[]
    for s in range(2):
        for c in range(2):
            e=gew_ref[s,c]
            pe[s,0,c]=jnp.where(low,e[0:192],pltpu.roll(e[192:384],64,1))
            pe[s,1,c]=jnp.where(low,pltpu.roll(e[0:192],64,1),e[192:384])
        for h in range(2):
            u=gco_ref[s,0,64*h:64*h+64]; v=gco_ref[s,1,64*h:64*h+64]
            pc[s,2*h]=jnp.where(low,u,pltpu.roll(v,64,1))
            pc[s,2*h+1]=jnp.where(low,pltpu.roll(u,64,1),v)
    s1.wait_recv()
    for j in range(8):
        w1[j]=half[32*j:32*j+32]+pg_ref[core,32*j:32*j+32]
    st=[send(w1.at[r],q1.at[7-k],(r,b)) for k,r in enumerate(rows)]
    for s in range(2):
        ret.append(send(gns_ref.at[s,:,0:64,:],rns.at[s,:,0:64,:],(dn,b)))
        ret.append(send(gns_ref.at[s,:,64:128,:],rns.at[s,:,64:128,:],(up,b)))
        ret.append(send(pe.at[s,0],rew.at[s,0],(a,rt)))
        ret.append(send(pe.at[s,1],rew.at[s,1],(a,lf)))
        for h,rr in ((0,dn),(1,up)):
            for l,cc in ((0,rt),(1,lf)):
                ret.append(send(pc.at[s,2*h+l],rco.at[s,2*h+l],(rr,cc)))
    out_ref[...]=gt_ref[...]
    for c in st: c.wait_recv()
    t=w1[a]
    for k in range(1,8): t=t+q1[k]
    for j in range(4): w2[j]=t[8*j:8*j+8]
    st=[send(w2.at[xx],q2.at[3-k],(a,xx*8+lax.rem(b,8))) for k,xx in enumerate(xs)]
    for c in st: c.wait_recv()
    t=w2[x]
    for k in range(1,4): t=t+q2[k]
    w3[...]=t
    st=[send(w3,q3.at[zh],(a,x*8+zz*2+core)) for zz in zs]
    q3[zh]=t
    for c in st: c.wait_recv()
    t=((q3[0]+q3[1])+(q3[2]+q3[3]))*scale
    ag2[x]=t
    st=[send(ag2.at[x],ag2.at[x],(a,xx*8+lax.rem(b,8))) for xx in xs]
    for c in st: c.wait_recv()
    for j in range(4): pout_ref[core,a,8*j:8*j+8]=ag2[j]
    st=[send(pout_ref.at[core,a],pout_ref.at[core,a],(r,b)) for r in rows]
    for c in ret: c.wait_recv()
    for s in range(2):
        for c in range(2):
            o=out_ref.at[s,c]
            o[0:64,:]+=rns[s,c,0:64]
            o[TILE-64:TILE,:]+=rns[s,c,64:128]
            p0=rew[s,0,c]; p1=rew[s,1,c]
            z=jnp.zeros_like(p0)
            o[0:192,0:128]+=jnp.where(low,p0,z)
            o[192:384,0:128]+=jnp.where(low,pltpu.roll(p0,64,1),z)
            o[0:192,256:384]+=jnp.where(low,z,pltpu.roll(p1,64,1))
            o[192:384,256:384]+=jnp.where(low,z,p1)
            for h in range(2):
                r0=(TILE-64)*h; z=jnp.zeros((64,128),F32)
                u=rco[s,2*h]; v=rco[s,2*h+1]
                if c==1: u=pltpu.roll(u,64,1)
                if c==0: v=pltpu.roll(v,64,1)
                o[r0:r0+64,0:128]+=jnp.where(low,u,z)
                o[r0:r0+64,256:384]+=jnp.where(low,z,v)
    for c in st: c.wait_recv()
    last=send(pout_ref.at[core],pout_ref.at[core],(a,mate))
    last.wait_recv()
    for c in pend: c.wait_send()


def returned(scale,gt,gns,gew,gco,pg):
    V=pl.BlockSpec(memory_space=pltpu.VMEM)
    n=41
    M=lambda *s: pltpu.VMEM(s,F32)
    return pl.pallas_call(functools.partial(return_kernel,scale),
        out_shape=[jax.ShapeDtypeStruct((2,2,TILE,TILE),F32),jax.ShapeDtypeStruct((2,8,32,N),F32)],
        in_specs=[V]*5,out_specs=[V]*2,
        scratch_shapes=[M(2,2,2,192,128),M(2,4,64,128),M(2,2,128,TILE),M(2,2,2,192,128),M(2,4,64,128),
            M(N,N),M(8,32,N),M(8,32,N),M(4,8,N),M(4,8,N),M(8,N),M(4,8,N),M(4,8,N),
            pltpu.SemaphoreType.DMA((n,)),pltpu.SemaphoreType.DMA((n,))],
        compiler_params=pltpu.CompilerParams(collective_id=1,has_side_effects=True,vmem_limit_bytes=50<<20),
    )(gt,gns,gew,gco,pg)


def local(object_field, offsets, amplitudes, probe, phase):
    ns,ew,co=halos(object_field)
    gt,gns,gew,gco,pg=compute(offsets.reshape(POS,2),object_field,ns,ew,co,amplitudes.reshape(POS,N,N),probe,phase)
    everyone=POS*lax.axis_size("row")*lax.axis_size("col")
    og,pg=returned(1.0/math.sqrt(everyone),gt,gns,gew,gco,pg)
    return og,pg.reshape(2,N,N)


def solution(mesh):
    in_specs=(P(None,None,"row","col"),P("row","col",None),P("row","col",None,None),P(),P())
    out_specs=(P(None,None,"row","col"),P())
    return jax.shard_map(local,mesh=mesh,in_specs=in_specs,out_specs=out_specs,check_vma=False)
```

time: 554 us -> 126 us (0.23); the launches traced: 545 us -> 125 us
  waiting for transfers between devices: 253 us -> 0 us
  local copies, waits for them, and re-layouts: 154 us -> 13.8 us
  Pallas kernels: 0 us -> 111 us
  matrix products: 54.7 us -> 0 us
  other arithmetic: 38.1 us -> 0 us
  loops' own time: 16 us -> 0 us
  starting transfers between devices: 14.7 us -> 0 us
  between operations: 14.7 us -> 0.66 us
    psum x1 -> x0, waiting for transfers between devices: 239 us -> none  [in_one(): subtotal = lax.psum(line, axis)]
    pallas_call x0 -> x3, Pallas kernels: none -> 111 us  [the longest x1 49.3 us: returned(): pl.pallas_call(functools.partial(return_kernel, scale), out_shape=[jax.Sh...]
    dot_general x12 -> x0, matrix products: 54.7 us -> none  [the longest x6 33.6 us: transform(): return jnp.einsum('pcnm,dckm->pdnk', first, table, precision=HIGH)]
    dynamic_update_slice x4 -> x0, local copies, waits for them, and re-layouts: 47.8 us -> none  [add_window(): lax.dynamic_update_slice(gathered, current + stacked[index], (0, 0, start...]
    gather x48 -> x0, local copies, waits for them, and re-layouts: 36.1 us -> none
    slice x13 -> x0, local copies, waits for them, and re-layouts: 22.9 us -> none  [the longest x3 4.63 us: in_one(): finished.append(subtotal[at:at + a.size].reshape(a.shape))]
    another operation x3 -> x0, loops' own time: 16 us -> none  [the longest x1 15.6 us: local(): lax.fori_loop(0, count, add_window, jnp.zeros((slices, 2, span, span), jn...]
    ppermute x8 -> x0, starting transfers between devices: 14.6 us -> none  [the longest x4 8.6 us: padded(): lax.ppermute(lax.slice_in_dim(block, 0, width, axis=dim), axis, backward)]
  transfers between devices with their start and end apart: 9 -> 0, of which waited for: 3 -> 0; matrix products, arithmetic and copies ran while one was open for 9% -> 0% of each run, Pallas kernels for 0% -> 0%
where the time goes in v1:
time: 126 us; the launch traced here: 125 us
  Pallas kernels  111 us (88%)
  local copies, waits for them, and re-layouts  13.8 us (11%)
    pallas_call x1, Pallas kernels, returned(): pl.pallas_call(functools.partial(return_kernel, scale), out_shape=[jax.Sh...  49.3 us
    pallas_call x1, Pallas kernels, halos(): pl.pallas_call(halo_kernel, out_shape=[jax.ShapeDtypeStruct(s, F32) for s...  31.4 us
    pallas_call x1, Pallas kernels, compute(): pl.pallas_call(compute_kernel, out_shape=[jax.ShapeDtypeStruct(s, F32) fo...  30.2 us
    unnamed x18, local copies, waits for them, and re-layouts  12.4 us

profile of v1, /device:TPU:1, one launch (start us, length us, event | category | flops | bytes accessed | tf_op | source)
XLA Modules:
  0.0 125.4 jit_solution(4785611056106340652)
XLA Ops:
  0.6 1.3 %copy.10.off_ref = s32[4,2]{1,0:T(4,128)} copy(s32[4,2]{0,1:T(2,128)} %bitcast.5) | data formatting | bytes 64 | tf_op jit(solution)/shard_map/reshape | solution.py:319
  2.0 0.0 copy-start
  2.0 1.7 %copy-done = f32[2,2,384,384]{3,2,1,0:T(8,128)S(1)} copy-done((f32[2,2,384,384]{3,2,1,0:T(8,128)S(1)}, f32[2,2,384,384]{3,2,1,0:T(8,128)}, u32[]{:S(2)}) %copy-start) | copy-done | bytes 2359320
  3.6 31.4 %shard_map.95 = (f32[2,2,128,384]{3,2,1,0:T(8,128)S(1)}, f32[2,2,2,192,128]{4,3,2,1,0:T(8,128)S(1)}, f32[2,4,64,128]{3,2,1,0:T(8,128)S(1)}) custom-call(f32[2,2,384,384]{3,2,1,0:T(8,128)S(1)} %copy-done), custom_call_target="tpu_custom_call" | custom-call | tf_op jit(solution)/shard_map/pallas_call | solution.py:209
  35.1 0.0 copy-start.3
  35.1 0.9 copy-done.3
  36.0 0.0 copy-start.4
  36.0 0.9 copy-done.4
  36.9 0.0 copy-start.7
  36.9 0.7 copy-done.7
  37.6 30.2 %shard_map.96 = (f32[2,2,384,384]{3,2,1,0:T(8,128)}, f32[2,2,128,384]{3,2,1,0:T(8,128)}, f32[2,2,384,128]{3,2,1,0:T(8,128)}, f32[2,2,128,128]{3,2,1,0:T(8,128)}, f32[2,256,256]{2,1,0:T(8,128)}) custom-call(s32[4,2]{1,0:T(4,128)} %copy.10.off_ref, f32[2,2,384,384]{3,2,1,0:T(8,128)} %obj_ref.3, f32[2,2,128,384]{3,2,1,0:T(8,128)} %copy-done.3, ...), custom_call_target="tpu_custom_call" | custom-call | tf_op jit(solution)/shard_map/pallas_call | solution.py:148
  67.8 0.0 copy-start.1
  67.8 1.1 copy-done.1
  68.9 0.0 copy-start.2
  68.9 1.1 copy-done.2
  70.1 0.0 copy-start.5
  70.1 1.0 copy-done.5
  71.1 0.0 copy-start.6
  71.1 0.9 copy-done.6
  72.0 49.3 %shard_map.97 = (f32[2,2,384,384]{3,2,1,0:T(8,128)}, f32[2,8,32,256]{3,2,1,0:T(8,128)S(1)}) custom-call(f32[2,2,384,384]{3,2,1,0:T(8,128)} %get-tuple-element.15.gt_ref, f32[2,2,128,384]{3,2,1,0:T(8,128)S(1)} %copy-done.1, f32[2,2,384,128]{3,2,1,0:T(8,128)S(1)} %copy-done.2, f32[2,2,128,128]{3,2,1,0:T(8,128)S(1)} %copy-done.6, f32[2,256,256]{2,1,0:T(8,128)S(1)} %copy-done.5), custom_call_target="tpu_custom_call" | custom-call | tf_op jit(solution)/shard_map/pallas_call | solution.py:307
  121.3 3.2 %copy.13 = f32[2,2,384,384]{3,2,1,0:T(8,128)} copy(f32[2,2,384,384]{3,2,1,0:T(8,128)} %get-tuple-element.24) | data formatting | bytes 4718592
  124.6 0.8 copy.14
Async XLA Ops:
  2.0 1.7 %copy-start = (f32[2,2,384,384]{3,2,1,0:T(8,128)S(1)}, f32[2,2,384,384]{3,2,1,0:T(8,128)}, u32[]{:S(2)}) copy-start(f32[2,2,384,384]{3,2,1,0:T(8,128)} %obj_ref.3) | copy-start | bytes 7077892
  35.1 0.9 copy-start.3
  36.0 0.9 copy-start.4
  36.9 0.7 copy-start.7
  67.8 1.1 copy-start.1
  68.9 1.1 copy-start.2
  70.1 1.0 copy-start.5
  71.1 0.9 copy-start.6

commit v2 on v1

v2 whole, which is shorter than its diff:
```python
import math, functools
import numpy as np
import jax, jax.numpy as jnp
from jax import lax
from jax.experimental import pallas as pl
from jax.experimental.pallas import tpu as pltpu
import ml_dtypes
from jax.sharding import PartitionSpec as P

TILE=384; HALO=64; N=256; H=128; POS=4
F32=jnp.float32; BF=jnp.bfloat16

def tables():
    k=np.arange(H)[:,None].astype(np.int64); n=np.arange(H)[None,:].astype(np.int64)
    out=[]
    for odd in (0,1):
        ang=-2*np.pi*(((2*k+odd)*n)%N)/N
        c=np.cos(ang)/16; s=np.sin(ang)/16
        out.append(np.block([[c,-s],[s,c]]))
    fe,fo=out
    t=np.stack([fe,fo,fe.T,fo.T]).astype(np.float32)
    hi=t.astype(ml_dtypes.bfloat16)
    lo=(t-hi.astype(np.float32)).astype(ml_dtypes.bfloat16)
    perm=np.zeros((N,N),np.float32)
    idx=np.concatenate([np.arange(0,N,2),np.arange(1,N,2)])
    perm[np.arange(N),idx]=1
    pm=np.stack([perm,perm.T]).astype(ml_dtypes.bfloat16)
    return hi,lo,pm

def split(x):
    hi=x.astype(BF); lo=(x-hi.astype(F32)).astype(BF)
    return hi,lo

def mm(a,b):
    return jnp.dot(a,b,preferred_element_type=F32)

def left(th,tl,x):
    xh,xl=split(x)
    return mm(jnp.concatenate([th,th,tl],1), jnp.concatenate([xh,xl,xh],0))
def right(x,th,tl):
    xh,xl=split(x)
    return mm(jnp.concatenate([xh,xl,xh],1), jnp.concatenate([th,th,tl],0))

def fwd(t,re,im):
    hi,lo=t
    a=jnp.concatenate([re[:H]+re[H:],im[:H]+im[H:]],0)
    b=jnp.concatenate([re[:H]-re[H:],im[:H]-im[H:]],0)
    ye=left(hi[0],lo[0],a); yo=left(hi[1],lo[1],b)
    re=jnp.concatenate([ye[:H],yo[:H]],0); im=jnp.concatenate([ye[H:],yo[H:]],0)
    a=jnp.concatenate([re[:,:H]+re[:,H:],im[:,:H]+im[:,H:]],1)
    b=jnp.concatenate([re[:,:H]-re[:,H:],im[:,:H]-im[:,H:]],1)
    ye=right(a,hi[2],lo[2]); yo=right(b,hi[3],lo[3])
    return jnp.concatenate([ye[:,:H],yo[:,:H]],1), jnp.concatenate([ye[:,H:],yo[:,H:]],1)

def inv(t,re,im):
    hi,lo=t
    u=right(jnp.concatenate([re[:,:H],im[:,:H]],1),hi[0],lo[0])
    v=right(jnp.concatenate([re[:,H:],im[:,H:]],1),hi[1],lo[1])
    s=u+v; d=u-v
    re=jnp.concatenate([s[:,:H],d[:,:H]],1); im=jnp.concatenate([s[:,H:],d[:,H:]],1)
    u=left(hi[2],lo[2],jnp.concatenate([re[:H],im[:H]],0))
    v=left(hi[3],lo[3],jnp.concatenate([re[H:],im[H:]],0))
    s=u+v; d=u-v
    return jnp.concatenate([s[:H],d[:H]],0), jnp.concatenate([s[H:],d[H:]],0)

def split3(x):
    h=x.astype(BF); r=x-h.astype(F32); m=r.astype(BF); l=(r-m.astype(F32)).astype(BF)
    return h,m,l
def permute(pm,x):
    h,m,l=split3(x)
    y=mm(pm[0],h)+mm(pm[0],m)+mm(pm[0],l)
    h,m,l=split3(y)
    return mm(h,pm[1])+mm(m,pm[1])+mm(l,pm[1])


MESH=pl.DeviceIdType.MESH


def greet(partners):
    bar=pltpu.get_barrier_semaphore()
    for d in partners:
        pl.semaphore_signal(bar,inc=1,device_id=d,device_id_type=MESH)
    return lambda: pl.semaphore_wait(bar,len(partners))


def fused_kernel(scale, off_ref, obj_ref, amp_ref, probe_ref, phase_ref, hi_ref, lo_ref, pm_ref,
                 out_ref, pout_ref,
                 ext, gext, amp, prb, phs, hi, lo, pm, hc, hs, rpr, wave, pg,
                 ns, ew, co, pe, pc, rns, rew, rco, qe, qc,
                 half, w1, q1, w2, q2, w3, q3, ag2, lsem, ssem, rsem):
    a=lax.axis_index("row"); b=lax.axis_index("col")
    nr=lax.axis_size("row"); nc=lax.axis_size("col")
    up=lax.rem(a+nr-1,nr); dn=lax.rem(a+1,nr); lf=lax.rem(b+nc-1,nc); rt=lax.rem(b+1,nc)
    core=lax.rem(b,2); zh=lax.rem(b//2,4); x=b//8
    mate=b+1-2*core
    rows=[lax.rem(a+k,nr) for k in range(1,8)]
    xs=[lax.rem(x+k,4) for k in range(1,4)]
    zs=[lax.rem(zh+k,4) for k in range(1,4)]
    low=lax.broadcasted_iota(jnp.int32,(1,128),1)<64
    met=greet([(r,b) for r in rows]+[(a,lf),(a,rt),(up,lf),(up,rt),(dn,lf),(dn,rt)]
          +[(a,xx*8+lax.rem(b,8)) for xx in xs]+[(a,x*8+zz*2+core) for zz in zs])
    loads=[]
    def load(src,dst):
        c=pltpu.make_async_copy(src,dst,lsem.at[len(loads)]); c.start(); loads.append(c)
        return c
    tiles=[load(obj_ref.at[s],ext.at[s,:,0:TILE,0:TILE]) for s in range(2)]
    small=[load(phase_ref,phs),load(pm_ref,pm),load(amp_ref,amp),load(probe_ref,prb),load(hi_ref,hi),load(lo_ref,lo)]
    count=[0]; pend=[]
    def send(src,dst,dev):
        i=count[0]; count[0]+=1
        c=pltpu.make_async_remote_copy(src,dst,ssem.at[i],rsem.at[i],device_id=dev,device_id_type=MESH)
        c.start(); pend.append(c)
        return c

    def pack(s):
        for c in range(2):
            e=ext.at[s,c]
            pe[s,0,c]=jnp.where(low,e[0:192,0:128],pltpu.roll(e[192:384,0:128],64,1))
            pe[s,1,c]=jnp.where(low,pltpu.roll(e[0:192,256:384],64,1),e[192:384,256:384])
        for h in range(2):
            r0=(TILE-64)*h
            u=ext.at[s,0]; v=ext.at[s,1]
            pc[s,2*h]=jnp.where(low,u[r0:r0+64,0:128],pltpu.roll(v[r0:r0+64,0:128],64,1))
            pc[s,2*h+1]=jnp.where(low,pltpu.roll(u[r0:r0+64,256:384],64,1),v[r0:r0+64,256:384])
    def give(s):
        out=[send(ext.at[s,:,0:64,0:TILE],ns.at[s,:,0:64,:],(up,b)),
             send(ext.at[s,:,TILE-64:TILE,0:TILE],ns.at[s,:,64:128,:],(dn,b)),
             send(pe.at[s,0],ew.at[s,0],(a,lf)),send(pe.at[s,1],ew.at[s,1],(a,rt))]
        for h,rr in ((0,up),(1,dn)):
            for l,cc in ((0,lf),(1,rt)):
                out.append(send(pc.at[s,2*h+l],co.at[s,2*h+l],(rr,cc)))
        return out
    def take(s):
        for c in range(2):
            e=ext.at[s,c]
            e[TILE:512,0:TILE]=ns[s,c]
            p0=ew[s,0,c]; p1=ew[s,1,c]
            e[0:192,TILE:512]=jnp.where(low,p0,pltpu.roll(p1,64,1))
            e[192:384,TILE:512]=jnp.where(low,pltpu.roll(p0,64,1),p1)
            for h in range(2):
                cr=co[s,2*h]; cl=co[s,2*h+1]
                if c==0: cl=pltpu.roll(cl,64,1)
                else: cr=pltpu.roll(cr,64,1)
                e[TILE+64*h:TILE+64*h+64,TILE:512]=jnp.where(low,cr,cl)
    def gpack(s):
        for c in range(2):
            e=gext.at[s,c]
            qe[s,0,c]=jnp.where(low,e[0:192,TILE:512],pltpu.roll(e[192:384,TILE:512],64,1))
            qe[s,1,c]=jnp.where(low,pltpu.roll(e[0:192,TILE:512],64,1),e[192:384,TILE:512])
        for h in range(2):
            r0=TILE+64*h
            u=gext[s,0,r0:r0+64,TILE:512]; v=gext[s,1,r0:r0+64,TILE:512]
            qc[s,2*h]=jnp.where(low,u,pltpu.roll(v,64,1))
            qc[s,2*h+1]=jnp.where(low,pltpu.roll(u,64,1),v)
    def ggive(s):
        out=[send(gext.at[s,:,TILE:TILE+64,0:TILE],rns.at[s,:,0:64,:],(dn,b)),
             send(gext.at[s,:,TILE+64:512,0:TILE],rns.at[s,:,64:128,:],(up,b)),
             send(qe.at[s,0],rew.at[s,0],(a,rt)),send(qe.at[s,1],rew.at[s,1],(a,lf))]
        for h,rr in ((0,dn),(1,up)):
            for l,cc in ((0,rt),(1,lf)):
                out.append(send(qc.at[s,2*h+l],rco.at[s,2*h+l],(rr,cc)))
        return out
    def gtake(s):
        for c in range(2):
            o=out_ref.at[s,c]
            o[0:64,:]+=rns[s,c,0:64]
            o[TILE-64:TILE,:]+=rns[s,c,64:128]
            p0=rew[s,0,c]; p1=rew[s,1,c]
            z=jnp.zeros_like(p0)
            o[0:192,0:128]+=jnp.where(low,p0,z)
            o[192:384,0:128]+=jnp.where(low,pltpu.roll(p0,64,1),z)
            o[0:192,256:384]+=jnp.where(low,z,pltpu.roll(p1,64,1))
            o[192:384,256:384]+=jnp.where(low,z,p1)
            for h in range(2):
                r0=(TILE-64)*h; z=jnp.zeros((64,128),F32)
                u=rco[s,2*h]; v=rco[s,2*h+1]
                if c==1: u=pltpu.roll(u,64,1)
                if c==0: v=pltpu.roll(v,64,1)
                o[r0:r0+64,0:128]+=jnp.where(low,u,z)
                o[r0:r0+64,256:384]+=jnp.where(low,z,v)

    tiles[0].wait(); pack(0)
    tiles[1].wait(); pack(1)
    met()
    got0=give(0)
    got1=give(1)
    gext[...]=jnp.zeros_like(gext)
    pg[...]=jnp.zeros_like(pg)
    for c in small: c.wait()
    pms=(pm[0],pm[1])
    ph=permute(pms,phs[...])
    hc[...]=jnp.cos(ph); hs[...]=jnp.sin(ph)
    def spot(p):
        r=off_ref[p,0,0]; c=off_ref[p,0,1]
        return r,c,lax.rem(r+192,N),lax.rem(c+192,N)
    def roll(v,i,j):
        return pltpu.roll(pltpu.roll(v,i,0),j,1)
    def ready(p,_):
        r,c,sr,sc=spot(p)
        amp[p]=permute(pms,amp[p])
        rpr[p,0]=roll(prb[0],sr,sc); rpr[p,1]=roll(prb[1],sr,sc)
        return 0
    lax.fori_loop(0,POS,ready,0)
    t=([hi[i] for i in range(4)],[lo[i] for i in range(4)])
    ri=lax.broadcasted_iota(jnp.int32,(N,1),0); ci=lax.broadcasted_iota(jnp.int32,(1,N),1)
    def masks(p):
        r,c,_,_=spot(p)
        return (jnp.broadcast_to((ri>=r-64)&(ri<r+192),(N,N)),jnp.broadcast_to((ci>=c-64)&(ci<c+192),(N,N)))
    def window(m,s,k):
        e=ext.at[s,k]; rm,cm=m
        return jnp.where(rm,jnp.where(cm,e[0:N,0:N],e[0:N,N:512]),jnp.where(cm,e[N:512,0:N],e[N:512,N:512]))
    def scatter(m,s,k,g):
        e=gext.at[s,k]; rm,cm=m
        z=jnp.zeros_like(g)
        gr=jnp.where(rm,g,z); gb=jnp.where(rm,z,g)
        e[0:N,0:N]+=jnp.where(cm,gr,z); e[0:N,N:512]+=jnp.where(cm,z,gr)
        e[N:512,0:N]+=jnp.where(cm,gb,z); e[N:512,N:512]+=jnp.where(cm,z,gb)
    def pairs(one):
        def body(i,_):
            one(2*i); one(2*i+1)
            return 0
        lax.fori_loop(0,POS//2,body,0)

    for c in got0: c.wait_recv()
    take(0)
    def first(p):
        m=masks(p)
        pr=rpr[p,0]; pi=rpr[p,1]
        wr=window(m,0,0); wi=window(m,0,1)
        fr,fi=fwd(t,pr*wr-pi*wi,pr*wi+pi*wr)
        cc=hc[...]; ss=hs[...]
        wave[p,0],wave[p,1]=inv(t,fr*cc-fi*ss,fr*ss+fi*cc)
    pairs(first)

    for c in got1: c.wait_recv()
    take(1)
    def second(p):
        m=masks(p)
        qr=wave[p,0]; qi=wave[p,1]
        wr=window(m,1,0); wi=window(m,1,1)
        fr,fi=fwd(t,qr*wr-qi*wi,qr*wi+qi*wr)
        keep=1.0-amp[p]*lax.rsqrt(jnp.maximum(fr*fr+fi*fi,0.25))
        br,bi=inv(t,fr*keep,fi*keep)
        scatter(m,1,0,qr*br+qi*bi); scatter(m,1,1,qr*bi-qi*br)
        wave[p,0]=wr*br+wi*bi; wave[p,1]=wr*bi-wi*br
    pairs(second)
    gpack(1)
    ret1=ggive(1)

    def third(p):
        m=masks(p)
        r,c,sr,sc=spot(p)
        fr,fi=fwd(t,wave[p,0],wave[p,1])
        cc=hc[...]; ss=hs[...]
        br,bi=inv(t,fr*cc+fi*ss,fi*cc-fr*ss)
        wr=window(m,0,0); wi=window(m,0,1)
        ur=lax.rem(N-sr,N); uc=lax.rem(N-sc,N)
        pg[0]+=roll(wr*br+wi*bi,ur,uc)
        pg[1]+=roll(wr*bi-wi*br,ur,uc)
        pr=rpr[p,0]; pi=rpr[p,1]
        wave[p,0]=pr*br+pi*bi; wave[p,1]=pr*bi-pi*br
    pairs(third)

    s1=send(pg.at[1-core],half,(a,mate))
    def fold(p,_):
        m=masks(p)
        for k in range(2): scatter(m,0,k,wave[p,k])
        return 0
    lax.fori_loop(0,POS,fold,0)
    gpack(0)
    s1.wait_recv()
    for j in range(8):
        w1[j]=half[32*j:32*j+32]+pg[core,32*j:32*j+32]
    st=[send(w1.at[r],q1.at[7-k],(r,b)) for k,r in enumerate(rows)]
    ret0=ggive(0)
    for s in range(2):
        for c in range(2):
            out_ref[s,c]=gext[s,c,0:TILE,0:TILE]
    for c in st: c.wait_recv()
    v=w1[a]
    for k in range(1,8): v=v+q1[k]
    for j in range(4): w2[j]=v[8*j:8*j+8]
    st=[send(w2.at[xx],q2.at[3-k],(a,xx*8+lax.rem(b,8))) for k,xx in enumerate(xs)]
    for c in st: c.wait_recv()
    v=w2[x]
    for k in range(1,4): v=v+q2[k]
    w3[...]=v
    st=[send(w3,q3.at[zh],(a,x*8+zz*2+core)) for zz in zs]
    q3[zh]=v
    for c in st: c.wait_recv()
    v=((q3[0]+q3[1])+(q3[2]+q3[3]))*scale
    ag2[x]=v
    st=[send(ag2.at[x],ag2.at[x],(a,xx*8+lax.rem(b,8))) for xx in xs]
    for c in ret1: c.wait_recv()
    gtake(1)
    for c in st: c.wait_recv()
    for j in range(4): pout_ref[core,a,8*j:8*j+8]=ag2[j]
    st=[send(pout_ref.at[core,a],pout_ref.at[core,a],(r,b)) for r in rows]
    for c in ret0: c.wait_recv()
    gtake(0)
    for c in st: c.wait_recv()
    last=send(pout_ref.at[core],pout_ref.at[core],(a,mate))
    last.wait_recv()
    for c in pend: c.wait_send()


def fused(scale,off,obj,amp,probe,phase):
    h,l,m=tables()
    V=pl.BlockSpec(memory_space=pltpu.VMEM); B=pl.BlockSpec(memory_space=pltpu.HBM)
    M=lambda *s: pltpu.VMEM(s,F32)
    n=57
    return pl.pallas_call(functools.partial(fused_kernel,scale),
        out_shape=[jax.ShapeDtypeStruct((2,2,TILE,TILE),F32),jax.ShapeDtypeStruct((2,8,32,N),F32)],
        in_specs=[pl.BlockSpec(memory_space=pltpu.SMEM)]+[B]*7,out_specs=[V]*2,
        scratch_shapes=[M(2,2,512,512),M(2,2,512,512),M(POS,N,N),M(2,N,N),M(N,N),pltpu.VMEM((4,N,N),BF),pltpu.VMEM((4,N,N),BF),
            pltpu.VMEM((2,N,N),BF),M(N,N),M(N,N),M(POS,2,N,N),M(POS,2,N,N),M(2,N,N),
            M(2,2,128,TILE),M(2,2,2,192,128),M(2,4,64,128),M(2,2,2,192,128),M(2,4,64,128),
            M(2,2,128,TILE),M(2,2,2,192,128),M(2,4,64,128),M(2,2,2,192,128),M(2,4,64,128),
            M(N,N),M(8,32,N),M(8,32,N),M(4,8,N),M(4,8,N),M(8,N),M(4,8,N),M(4,8,N),
            pltpu.SemaphoreType.DMA((8,)),pltpu.SemaphoreType.DMA((n,)),pltpu.SemaphoreType.DMA((n,))],
        compiler_params=pltpu.CompilerParams(collective_id=0,has_side_effects=True,vmem_limit_bytes=48<<20),
    )(off,obj,amp,probe,phase,jnp.asarray(h),jnp.asarray(l),jnp.asarray(m))


def local(object_field, offsets, amplitudes, probe, phase):
    everyone=POS*lax.axis_size("row")*lax.axis_size("col")
    og,pgr=fused(1.0/math.sqrt(everyone),offsets,object_field,amplitudes.reshape(POS,N,N),probe,phase)
    return og,pgr.reshape(2,N,N)


def solution(mesh):
    in_specs=(P(None,None,"row","col"),P("row","col",None),P("row","col",None,None),P(),P())
    out_specs=(P(None,None,"row","col"),P())
    return jax.shard_map(local,mesh=mesh,in_specs=in_specs,out_specs=out_specs,check_vma=False)
```

time: 126 us -> 88.7 us (0.70)
  Pallas kernels: 111 us -> 78.5 us
  local copies, waits for them, and re-layouts: 13.8 us -> 9.21 us
    pallas_call x3 -> x1, Pallas kernels: 111 us -> 78.5 us  [fused(): pl.pallas_call(functools.partial(fused_kernel, scale), out_shape=[jax.Sha...]
    unnamed x18 -> x15, local copies, waits for them, and re-layouts: 12.4 us -> 9.21 us
    reshape x1 -> x0, local copies, waits for them, and re-layouts: 1.35 us -> none  [local(): offsets.reshape(POS, 2)]
where the time goes in v2:
time: 88.7 us; the launch traced here: 88.4 us
  Pallas kernels  78.5 us (89%)
  local copies, waits for them, and re-layouts  9.21 us (10%)
    pallas_call x1, Pallas kernels, fused(): pl.pallas_call(functools.partial(fused_kernel, scale), out_shape=[jax.Sha...  78.5 us
    unnamed x15, local copies, waits for them, and re-layouts  9.21 us

profile of v2, /device:TPU:1, one launch (start us, length us, event | category | flops | bytes accessed | tf_op | source)
XLA Modules:
  0.0 88.4 jit_solution(5563503134188826401)
XLA Ops:
  0.6 0.8 copy.10.off_ref
  1.4 0.0 copy-start
  1.4 1.2 %copy-done = f32[4,1,256,256]{3,2,1,0:T(8,128)S(1)} copy-done((f32[4,1,256,256]{3,2,1,0:T(8,128)S(1)}, f32[4,1,256,256]{3,2,1,0:T(8,128)}, u32[]{:S(2)}) %copy-start) | copy-done | bytes 1048600
  2.6 0.0 copy-start.1
  2.6 1.0 %copy-done.1 = f32[2,256,256]{2,1,0:T(8,128)S(1)} copy-done((f32[2,256,256]{2,1,0:T(8,128)S(1)}, f32[2,256,256]{2,1,0:T(8,128)}, u32[]{:S(2)}) %copy-start.1) | copy-done | bytes 524312
  3.7 0.0 copy-start.2
  3.7 1.0 %copy-done.2 = bf16[4,256,256]{2,1,0:T(8,128)(2,1)S(1)} copy-done((bf16[4,256,256]{2,1,0:T(8,128)(2,1)S(1)}, bf16[4,256,256]{2,1,0:T(8,128)(2,1)}, u32[]{:S(2)}) %copy-start.2) | copy-done | bytes 524312
  4.7 0.0 copy-start.3
  4.7 1.0 %copy-done.3 = bf16[4,256,256]{2,1,0:T(8,128)(2,1)S(1)} copy-done((bf16[4,256,256]{2,1,0:T(8,128)(2,1)S(1)}, bf16[4,256,256]{2,1,0:T(8,128)(2,1)}, u32[]{:S(2)}) %copy-start.3) | copy-done | bytes 524312
  5.7 0.0 copy-start.4
  5.7 0.9 %copy-done.4 = f32[256,256]{1,0:T(8,128)S(1)} copy-done((f32[256,256]{1,0:T(8,128)S(1)}, f32[256,256]{1,0:T(8,128)}, u32[]{:S(2)}) %copy-start.4) | copy-done | bytes 262168
  6.7 0.0 copy-start.5
  6.7 0.9 %copy-done.5 = bf16[2,256,256]{2,1,0:T(8,128)(2,1)S(1)} copy-done((bf16[2,256,256]{2,1,0:T(8,128)(2,1)S(1)}, bf16[2,256,256]{2,1,0:T(8,128)(2,1)}, u32[]{:S(2)}) %copy-start.5) | copy-done | bytes 262168
  7.6 78.5 %shard_map.95 = (f32[2,2,384,384]{3,2,1,0:T(8,128)S(1)}, f32[2,8,32,256]{3,2,1,0:T(8,128)S(1)}) custom-call(s32[4,1,2]{2,1,0:T(1,128)S(1)} %copy.10.off_ref, f32[2,2,384,384]{3,2,1,0:T(8,128)} %obj_ref.1, f32[4,256,256]{2,1,0:T(8,128)S(1)} %bitcast.2, f32[2,256,256]{2,1,0:T(8,128)S(1)} %copy-done.1, f32[256,256]{1,0:T(8,128)S(1)} %copy-done.4, ...), custom_call_target="tpu_custom_call" | custom-call | tf_op jit(solution)/shard_map/pallas_call | solution.py:312
  86.2 1.4 %copy.13 = f32[2,2,384,384]{3,2,1,0:T(8,128)} copy(f32[2,2,384,384]{3,2,1,0:T(8,128)S(1)} %get-tuple-element.8) | data formatting | bytes 4718592
  87.6 0.8 copy.14
Async XLA Ops:
  1.4 1.2 %copy-start = (f32[4,1,256,256]{3,2,1,0:T(8,128)S(1)}, f32[4,1,256,256]{3,2,1,0:T(8,128)}, u32[]{:S(2)}) copy-start(f32[4,1,256,256]{3,2,1,0:T(8,128)} %param.10) | copy-start | bytes 3145732
  2.6 1.0 %copy-start.1 = (f32[2,256,256]{2,1,0:T(8,128)S(1)}, f32[2,256,256]{2,1,0:T(8,128)}, u32[]{:S(2)}) copy-start(f32[2,256,256]{2,1,0:T(8,128)} %probe_ref.1) | copy-start | bytes 1572868
  3.7 1.0 %copy-start.2 = (bf16[4,256,256]{2,1,0:T(8,128)(2,1)S(1)}, bf16[4,256,256]{2,1,0:T(8,128)(2,1)}, u32[]{:S(2)}) copy-start(bf16[4,256,256]{2,1,0:T(8,128)(2,1)} %constant.7.clone.lo_ref) | copy-start | bytes 1572868
  4.7 1.0 %copy-start.3 = (bf16[4,256,256]{2,1,0:T(8,128)(2,1)S(1)}, bf16[4,256,256]{2,1,0:T(8,128)(2,1)}, u32[]{:S(2)}) copy-start(bf16[4,256,256]{2,1,0:T(8,128)(2,1)} %constant.6.clone.hi_ref) | copy-start | bytes 1572868
  5.7 0.9 %copy-start.4 = (f32[256,256]{1,0:T(8,128)S(1)}, f32[256,256]{1,0:T(8,128)}, u32[]{:S(2)}) copy-start(f32[256,256]{1,0:T(8,128)} %phase_ref.1) | copy-start | bytes 786436
  6.7 0.9 %copy-start.5 = (bf16[2,256,256]{2,1,0:T(8,128)(2,1)S(1)}, bf16[2,256,256]{2,1,0:T(8,128)(2,1)}, u32[]{:S(2)}) copy-start(bf16[2,256,256]{2,1,0:T(8,128)(2,1)} %constant.8.clone.pm_ref) | copy-start | bytes 786436

commit v3 on v2

--- a/solution.py
+++ b/solution.py
@@ -1,31 +1,31 @@
 import math, functools
-import numpy as np
 import jax, jax.numpy as jnp
 from jax import lax
 from jax.experimental import pallas as pl
 from jax.experimental.pallas import tpu as pltpu
-import ml_dtypes
 from jax.sharding import PartitionSpec as P
 
 TILE=384; HALO=64; N=256; H=128; POS=4
 F32=jnp.float32; BF=jnp.bfloat16
 
-def tables():
-    k=np.arange(H)[:,None].astype(np.int64); n=np.arange(H)[None,:].astype(np.int64)
-    out=[]
-    for odd in (0,1):
-        ang=-2*np.pi*(((2*k+odd)*n)%N)/N
-        c=np.cos(ang)/16; s=np.sin(ang)/16
-        out.append(np.block([[c,-s],[s,c]]))
-    fe,fo=out
-    t=np.stack([fe,fo,fe.T,fo.T]).astype(np.float32)
-    hi=t.astype(ml_dtypes.bfloat16)
-    lo=(t-hi.astype(np.float32)).astype(ml_dtypes.bfloat16)
-    perm=np.zeros((N,N),np.float32)
-    idx=np.concatenate([np.arange(0,N,2),np.arange(1,N,2)])
-    perm[np.arange(N),idx]=1
-    pm=np.stack([perm,perm.T]).astype(ml_dtypes.bfloat16)
-    return hi,lo,pm
+def make_tables(hi,lo,pm):
+    k=lax.broadcasted_iota(jnp.int32,(H,H),0); n=lax.broadcasted_iota(jnp.int32,(H,H),1)
+    def wave(m):
+        t=jnp.bitwise_and(m,N-1).astype(F32)*(2.0*math.pi/N)
+        return jnp.cos(t)*0.0625,-jnp.sin(t)*0.0625
+    def put(i,c,s):
+        hi[i],lo[i]=split(jnp.concatenate([jnp.concatenate([c,-s],1),jnp.concatenate([s,c],1)],0))
+    c,s=wave(2*k*n)
+    put(0,c,s); put(2,c,-s)
+    c,s=wave((2*k+1)*n)
+    put(1,c,s)
+    c,s=wave((2*n+1)*k)
+    put(3,c,-s)
+    i=lax.broadcasted_iota(jnp.int32,(N,N),0); j=lax.broadcasted_iota(jnp.int32,(N,N),1)
+    def ones(u,v):
+        at=jnp.where(u<H,2*u,2*u-(N-1))
+        return jnp.where(v==at,1.0,0.0).astype(BF)
+    pm[0]=ones(i,j); pm[1]=ones(j,i)
 
 def split(x):
     hi=x.astype(BF); lo=(x-hi.astype(F32)).astype(BF)
@@ -83,11 +83,11 @@
     return lambda: pl.semaphore_wait(bar,len(partners))
 
 
-def fused_kernel(scale, off_ref, obj_ref, amp_ref, probe_ref, phase_ref, hi_ref, lo_ref, pm_ref,
+def fused_kernel(scale, offs_ref, obj_ref, amp_ref, probe_ref, phase_ref,
                  out_ref, pout_ref,
-                 ext, gext, amp, prb, phs, hi, lo, pm, hc, hs, rpr, wave, pg,
+                 off_ref, ext, gext, amp, prb, phs, hi, lo, pm, hc, hs, rpr, wave, pg,
                  ns, ew, co, pe, pc, rns, rew, rco, qe, qc,
-                 half, w1, q1, w2, q2, w3, q3, ag2, lsem, ssem, rsem):
+                 half, w1, q1, w2, q2, w3, q3, ag2, pf, lsem, ssem, rsem):
     a=lax.axis_index("row"); b=lax.axis_index("col")
     nr=lax.axis_size("row"); nc=lax.axis_size("col")
     up=lax.rem(a+nr-1,nr); dn=lax.rem(a+1,nr); lf=lax.rem(b+nc-1,nc); rt=lax.rem(b+1,nc)
@@ -104,7 +104,7 @@
         c=pltpu.make_async_copy(src,dst,lsem.at[len(loads)]); c.start(); loads.append(c)
         return c
     tiles=[load(obj_ref.at[s],ext.at[s,:,0:TILE,0:TILE]) for s in range(2)]
-    small=[load(phase_ref,phs),load(pm_ref,pm),load(amp_ref,amp),load(probe_ref,prb),load(hi_ref,hi),load(lo_ref,lo)]
+    small=[load(phase_ref,phs),load(amp_ref,amp),load(probe_ref,prb),load(offs_ref,off_ref)]
     count=[0]; pend=[]
     def send(src,dst,dev):
         i=count[0]; count[0]+=1
@@ -162,9 +162,9 @@
         return out
     def gtake(s):
         for c in range(2):
-            o=out_ref.at[s,c]
-            o[0:64,:]+=rns[s,c,0:64]
-            o[TILE-64:TILE,:]+=rns[s,c,64:128]
+            o=gext.at[s,c]
+            o[0:64,0:TILE]+=rns[s,c,0:64]
+            o[TILE-64:TILE,0:TILE]+=rns[s,c,64:128]
             p0=rew[s,0,c]; p1=rew[s,1,c]
             z=jnp.zeros_like(p0)
             o[0:192,0:128]+=jnp.where(low,p0,z)
@@ -186,12 +186,13 @@
     got1=give(1)
     gext[...]=jnp.zeros_like(gext)
     pg[...]=jnp.zeros_like(pg)
+    make_tables(hi,lo,pm)
     for c in small: c.wait()
     pms=(pm[0],pm[1])
     ph=permute(pms,phs[...])
     hc[...]=jnp.cos(ph); hs[...]=jnp.sin(ph)
     def spot(p):
-        r=off_ref[p,0,0]; c=off_ref[p,0,1]
+        r=off_ref[0,p]; c=off_ref[1,p]
         return r,c,lax.rem(r+192,N),lax.rem(c+192,N)
     def roll(v,i,j):
         return pltpu.roll(pltpu.roll(v,i,0),j,1)
@@ -261,24 +262,22 @@
         wave[p,0]=pr*br+pi*bi; wave[p,1]=pr*bi-pi*br
     pairs(third)
 
-    s1=send(pg.at[1-core],half,(a,mate))
+    s1=[send(pg.at[1-core,pl.ds(pl.multiple_of(32*r,32),32)],half.at[k],(a,mate)) for k,r in enumerate(rows+[a])]
     def fold(p,_):
         m=masks(p)
         for k in range(2): scatter(m,0,k,wave[p,k])
         return 0
     lax.fori_loop(0,POS,fold,0)
     gpack(0)
-    s1.wait_recv()
-    for j in range(8):
-        w1[j]=half[32*j:32*j+32]+pg[core,32*j:32*j+32]
-    st=[send(w1.at[r],q1.at[7-k],(r,b)) for k,r in enumerate(rows)]
+    st=[]
+    for k,r in enumerate(rows+[a]):
+        s1[k].wait_recv()
+        w1[k]=half[k]+pg[core,pl.ds(pl.multiple_of(32*r,32),32)]
+        if k<7: st.append(send(w1.at[k],q1.at[6-k],(r,b)))
     ret0=ggive(0)
-    for s in range(2):
-        for c in range(2):
-            out_ref[s,c]=gext[s,c,0:TILE,0:TILE]
     for c in st: c.wait_recv()
-    v=w1[a]
-    for k in range(1,8): v=v+q1[k]
+    v=w1[7]
+    for k in range(7): v=v+q1[k]
     for j in range(4): w2[j]=v[8*j:8*j+8]
     st=[send(w2.at[xx],q2.at[3-k],(a,xx*8+lax.rem(b,8))) for k,xx in enumerate(xs)]
     for c in st: c.wait_recv()
@@ -293,39 +292,65 @@
     st=[send(ag2.at[x],ag2.at[x],(a,xx*8+lax.rem(b,8))) for xx in xs]
     for c in ret1: c.wait_recv()
     gtake(1)
+    outs=[load(gext.at[1,:,0:TILE,0:TILE],out_ref.at[1])]
     for c in st: c.wait_recv()
-    for j in range(4): pout_ref[core,a,8*j:8*j+8]=ag2[j]
-    st=[send(pout_ref.at[core,a],pout_ref.at[core,a],(r,b)) for r in rows]
+    for j in range(4): pf[core,a,8*j:8*j+8]=ag2[j]
+    st=[send(pf.at[core,a],pf.at[core,a],(r,b)) for r in rows]
+    fin=[send(pf.at[core,a],pf.at[core,a],(a,mate))]
     for c in ret0: c.wait_recv()
     gtake(0)
-    for c in st: c.wait_recv()
-    last=send(pout_ref.at[core],pout_ref.at[core],(a,mate))
-    last.wait_recv()
+    outs.append(load(gext.at[0,:,0:TILE,0:TILE],out_ref.at[0]))
+    for k in range(7):
+        st[k].wait_recv()
+        r=rows[6-k]
+        fin.append(send(pf.at[core,r],pf.at[core,r],(a,mate)))
+    outs.append(load(pf.at[core],pout_ref.at[core]))
+    for c in fin: c.wait_recv()
+    outs.append(load(pf.at[1-core],pout_ref.at[1-core]))
+    for c in outs: c.wait()
     for c in pend: c.wait_send()
 
 
 def fused(scale,off,obj,amp,probe,phase):
-    h,l,m=tables()
-    V=pl.BlockSpec(memory_space=pltpu.VMEM); B=pl.BlockSpec(memory_space=pltpu.HBM)
+    B=pl.BlockSpec(memory_space=pltpu.HBM)
     M=lambda *s: pltpu.VMEM(s,F32)
-    n=57
+    n=71
     return pl.pallas_call(functools.partial(fused_kernel,scale),
         out_shape=[jax.ShapeDtypeStruct((2,2,TILE,TILE),F32),jax.ShapeDtypeStruct((2,8,32,N),F32)],
-        in_specs=[pl.BlockSpec(memory_space=pltpu.SMEM)]+[B]*7,out_specs=[V]*2,
-        scratch_shapes=[M(2,2,512,512),M(2,2,512,512),M(POS,N,N),M(2,N,N),M(N,N),pltpu.VMEM((4,N,N),BF),pltpu.VMEM((4,N,N),BF),
+        in_specs=[B]*5,out_specs=[B]*2,
+        scratch_shapes=[pltpu.SMEM((2,POS),jnp.int32),M(2,2,512,512),M(2,2,512,512),M(POS,N,N),M(2,N,N),M(N,N),pltpu.VMEM((4,N,N),BF),pltpu.VMEM((4,N,N),BF),
             pltpu.VMEM((2,N,N),BF),M(N,N),M(N,N),M(POS,2,N,N),M(POS,2,N,N),M(2,N,N),
             M(2,2,128,TILE),M(2,2,2,192,128),M(2,4,64,128),M(2,2,2,192,128),M(2,4,64,128),
             M(2,2,128,TILE),M(2,2,2,192,128),M(2,4,64,128),M(2,2,2,192,128),M(2,4,64,128),
-            M(N,N),M(8,32,N),M(8,32,N),M(4,8,N),M(4,8,N),M(8,N),M(4,8,N),M(4,8,N),
-            pltpu.SemaphoreType.DMA((8,)),pltpu.SemaphoreType.DMA((n,)),pltpu.SemaphoreType.DMA((n,))],
-        compiler_params=pltpu.CompilerParams(collective_id=0,has_side_effects=True,vmem_limit_bytes=48<<20),
-    )(off,obj,amp,probe,phase,jnp.asarray(h),jnp.asarray(l),jnp.asarray(m))
+            M(8,32,N),M(8,32,N),M(7,32,N),M(4,8,N),M(4,8,N),M(8,N),M(4,8,N),M(4,8,N),M(2,8,32,N),
+            pltpu.SemaphoreType.DMA((10,)),pltpu.SemaphoreType.DMA((n,)),pltpu.SemaphoreType.DMA((n,))],
+        compiler_params=pltpu.CompilerParams(collective_id=0,has_side_effects=True,vmem_limit_bytes=58<<20),
+    )(off,obj,amp,probe,phase)
+
+
+def move_kernel(x_ref, y_ref, ox_ref, oy_ref, xb, yb, isem, osem):
+    parts=[(x_ref.at[i//2,i%2],xb.at[i//2,i%2],ox_ref.at[i//2,i%2]) for i in range(4)]+[(y_ref.at[i],yb.at[i],oy_ref.at[i]) for i in range(2)]
+    come=[pltpu.make_async_copy(u,v,isem.at[i]) for i,(u,v,_) in enumerate(parts)]
+    go=[pltpu.make_async_copy(v,w,osem.at[i]) for i,(_,v,w) in enumerate(parts)]
+    for c in come: c.start()
+    for c,g in zip(come,go):
+        c.wait(); g.start()
+    for g in go: g.wait()
+
+
+def move(x,y):
+    B=pl.BlockSpec(memory_space=pltpu.HBM)
+    return pl.pallas_call(move_kernel,
+        out_shape=[jax.ShapeDtypeStruct(x.shape,F32),jax.ShapeDtypeStruct(y.shape,F32)],
+        in_specs=[B]*2,out_specs=[B]*2,
+        scratch_shapes=[pltpu.VMEM(x.shape,F32),pltpu.VMEM(y.shape,F32),pltpu.SemaphoreType.DMA((6,)),pltpu.SemaphoreType.DMA((6,))],
+        compiler_params=pltpu.CompilerParams(vmem_limit_bytes=58<<20))(x,y)
 
 
 def local(object_field, offsets, amplitudes, probe, phase):
     everyone=POS*lax.axis_size("row")*lax.axis_size("col")
-    og,pgr=fused(1.0/math.sqrt(everyone),offsets,object_field,amplitudes.reshape(POS,N,N),probe,phase)
-    return og,pgr.reshape(2,N,N)
+    og,pgr=fused(1.0/math.sqrt(everyone),offsets.reshape(POS,2).T,object_field,amplitudes.reshape(POS,N,N),probe,phase)
+    return move(og,pgr.reshape(2,N,N))
 
 
 def solution(mesh):

time: 88.7 us -> 82.4 us (0.929)
  local copies, waits for them, and re-layouts: 9.21 us -> 0 us
  Pallas kernels: 78.5 us -> 81.4 us
    unnamed x15 -> x0, local copies, waits for them, and re-layouts: 9.21 us -> none
    pallas_call x0 -> x1, Pallas kernels: none -> 2.73 us  [move(): pl.pallas_call(move_kernel, out_shape=[jax.ShapeDtypeStruct(x.shape, F32)...]
where the time goes in v3:
time: 82.4 us; the launch traced here: 82.2 us
  Pallas kernels  81.4 us (99%)
    pallas_call x1, Pallas kernels, fused(): pl.pallas_call(functools.partial(fused_kernel, scale), out_shape=[jax.Sha...  78.7 us
    pallas_call x1, Pallas kernels, move(): pl.pallas_call(move_kernel, out_shape=[jax.ShapeDtypeStruct(x.shape, F32)...  2.73 us

profile of v3, /device:TPU:1, one launch (start us, length us, event | category | flops | bytes accessed | tf_op | source)
XLA Modules:
  0.0 82.2 jit_solution(12438522638984596127)
XLA Ops:
  0.6 78.7 %shard_map.68 = (f32[2,2,384,384]{3,2,1,0:T(8,128)}, f32[2,8,32,256]{3,2,1,0:T(8,128)}) custom-call(s32[2,4]{1,0:T(2,128)} %bitcast.7, f32[2,2,384,384]{3,2,1,0:T(8,128)} %obj_ref.1, f32[4,256,256]{2,1,0:T(8,128)} %bitcast.5, f32[2,256,256]{2,1,0:T(8,128)} %probe_ref.1, f32[256,256]{1,0:T(8,128)} %phase_ref.1), custom_call_target="tpu_custom_call" | custom-call | tf_op jit(solution)/shard_map/pallas_call | solution.py:318
  79.3 2.7 %shard_map.69 = (f32[2,2,384,384]{3,2,1,0:T(8,128)}, f32[2,256,256]{2,1,0:T(8,128)}) custom-call(f32[2,2,384,384]{3,2,1,0:T(8,128)} %get-tuple-element.4.x_ref, f32[2,256,256]{2,1,0:T(8,128)} %bitcast.6), custom_call_target="tpu_custom_call" | custom-call | tf_op jit(solution)/shard_map/pallas_call | solution.py:343

commit v4 on v3

--- a/solution.py
+++ b/solution.py
@@ -217,10 +217,7 @@
         e[0:N,0:N]+=jnp.where(cm,gr,z); e[0:N,N:512]+=jnp.where(cm,z,gr)
         e[N:512,0:N]+=jnp.where(cm,gb,z); e[N:512,N:512]+=jnp.where(cm,z,gb)
     def pairs(one):
-        def body(i,_):
-            one(2*i); one(2*i+1)
-            return 0
-        lax.fori_loop(0,POS//2,body,0)
+        for p in range(POS): one(p)
 
     for c in got0: c.wait_recv()
     take(0)
@@ -329,7 +326,8 @@
 
 
 def move_kernel(x_ref, y_ref, ox_ref, oy_ref, xb, yb, isem, osem):
-    parts=[(x_ref.at[i//2,i%2],xb.at[i//2,i%2],ox_ref.at[i//2,i%2]) for i in range(4)]+[(y_ref.at[i],yb.at[i],oy_ref.at[i]) for i in range(2)]
+    def cut(u,i): return u.at[i//6,i//3%2,i%3*128:i%3*128+128]
+    parts=[(cut(x_ref,i),cut(xb,i),cut(ox_ref,i)) for i in range(12)]+[(y_ref.at[i],yb.at[i],oy_ref.at[i]) for i in range(2)]
     come=[pltpu.make_async_copy(u,v,isem.at[i]) for i,(u,v,_) in enumerate(parts)]
     go=[pltpu.make_async_copy(v,w,osem.at[i]) for i,(_,v,w) in enumerate(parts)]
     for c in come: c.start()
@@ -343,7 +341,7 @@
     return pl.pallas_call(move_kernel,
         out_shape=[jax.ShapeDtypeStruct(x.shape,F32),jax.ShapeDtypeStruct(y.shape,F32)],
         in_specs=[B]*2,out_specs=[B]*2,
-        scratch_shapes=[pltpu.VMEM(x.shape,F32),pltpu.VMEM(y.shape,F32),pltpu.SemaphoreType.DMA((6,)),pltpu.SemaphoreType.DMA((6,))],
+        scratch_shapes=[pltpu.VMEM(x.shape,F32),pltpu.VMEM(y.shape,F32),pltpu.SemaphoreType.DMA((14,)),pltpu.SemaphoreType.DMA((14,))],
         compiler_params=pltpu.CompilerParams(vmem_limit_bytes=58<<20))(x,y)
 
 

time: 82.4 us -> 81.9 us (level)
  no operation moved by 1% of the time
where the time goes in v4:
time: 81.9 us; the launch traced here: 81.8 us
  Pallas kernels  81 us (99%)
  between operations  0.82 us (1%)
    pallas_call x1, Pallas kernels, fused(): pl.pallas_call(functools.partial(fused_kernel, scale), out_shape=[jax.Sha...  78.1 us
    pallas_call x1, Pallas kernels, move(): pl.pallas_call(move_kernel, out_shape=[jax.ShapeDtypeStruct(x.shape, F32)...  2.88 us

profile of v4, /device:TPU:1, one launch (start us, length us, event | category | flops | bytes accessed | tf_op | source)
XLA Modules:
  0.0 81.8 jit_solution(6444062698984509253)
XLA Ops:
  0.6 78.1 %shard_map.68 = (f32[2,2,384,384]{3,2,1,0:T(8,128)}, f32[2,8,32,256]{3,2,1,0:T(8,128)}) custom-call(s32[2,4]{1,0:T(2,128)} %bitcast.7, f32[2,2,384,384]{3,2,1,0:T(8,128)} %obj_ref.1, f32[4,256,256]{2,1,0:T(8,128)} %bitcast.5, f32[2,256,256]{2,1,0:T(8,128)} %probe_ref.1, f32[256,256]{1,0:T(8,128)} %phase_ref.1), custom_call_target="tpu_custom_call" | custom-call | tf_op jit(solution)/shard_map/pallas_call | solution.py:315
  78.7 2.9 %shard_map.69 = (f32[2,2,384,384]{3,2,1,0:T(8,128)}, f32[2,256,256]{2,1,0:T(8,128)}) custom-call(f32[2,2,384,384]{3,2,1,0:T(8,128)} %get-tuple-element.4.x_ref, f32[2,256,256]{2,1,0:T(8,128)} %bitcast.6), custom_call_target="tpu_custom_call" | custom-call | tf_op jit(solution)/shard_map/pallas_call | solution.py:341
